TPU v7x, 32 devices: a whole 2x2x4 slice. The times are simulated.
32 devices in a mesh: seq: 8 (over y, x, core), head: 4 (over z).
Axes of the slice: x: 2, y: 2, z: 4, core: 2. Of those that a mesh axis runs over, the one named last changes fastest.
Arguments:
- query_lin: bfloat16 [512, 4096], P('seq', 'head'), may hold values from -6 to 6
- key_lin: bfloat16 [512, 4096], P('seq', 'head'), may hold values from -6 to 6
- value_lin: bfloat16 [512, 4096], P('seq', 'head'), may hold values from -6 to 6
- log_decay: float32 [32, 512], P('head', 'seq'), may hold values from -1.6 to 0
- query_soft: bfloat16 [512, 4096], P(('seq', 'head')), may hold values from -4.5 to 4.5
- key_soft: bfloat16 [512, 512], P(('seq', 'head')), may hold values from -4.5 to 4.5
- value_soft: bfloat16 [512, 512], P(('seq', 'head')), may hold values from -6 to 6
- doc_start: int32 [512], P('seq'), may hold values from 0 to 480, as said below
Outputs:
- lin_out: bfloat16 [512, 4096], P('seq', 'head')
- soft_out: bfloat16 [512, 4096], P('seq', 'head')
- soft_lse: float32 [32, 512], P('head', 'seq')
Inputs may be any that keep to these rules, and one draw needn't show every extreme that they name: doc_start[t] is the first position of the document that holds token t: 0 for the first document, never above t, the same over a document; at most 4 documents; every document but the first and the last starts at a position of 1 to 32; the last document starts at 480.
All inputs are finite; a program needn't handle non-finite values.
Results may differ from a plain program's by a relative error of at most 0.003.
Values may be sent and summed in bfloat16 or wider, within the bound.
A program may use at most 256 MiB of HBM per device.

v0:
```python
import jax
import jax.numpy as jnp
from jax import lax
from jax.sharding import PartitionSpec as P

DH = 128


HIGHEST = lax.Precision.HIGHEST
masked_score = -1e30


def prefix(array, axis, combine, identity):
    size, here = (lax.axis_size(axis), lax.axis_index(axis))
    everything = jax.tree.map(lambda part: lax.all_gather(part, axis), array)
    start = jax.tree.map(
        lambda part, zero: jnp.broadcast_to(jnp.asarray(zero, part.dtype), part.shape),
        array,
        identity,
    )

    def lap(k, before):
        reached = k < here
        new = combine(before, jax.tree.map(lambda part: part[k], everything))
        return jax.tree.map(lambda a, b: jnp.where(reached, a, b), new, before)

    return lax.fori_loop(0, size, lap, start)


def span_terms(query_heads, key_heads, value_heads, decay_rows, doc_rows, first_place):
    span_len = query_heads.shape[0]
    cumulative = jnp.cumsum(decay_rows, axis=1)
    totals = cumulative[:, -1]
    token_positions = first_place + jnp.arange(span_len, dtype=jnp.int32)
    allowed = (token_positions[None, :] <= token_positions[:, None]) & (
        doc_rows[:, None] <= token_positions[None, :]
    )
    decay_gap = jnp.where(allowed[None], cumulative[:, :, None] - cumulative[:, None, :], 0.0)
    decay_mat = jnp.where(allowed[None], jnp.exp(decay_gap), 0.0)
    scores = jnp.einsum("thd,shd->hts", query_heads, key_heads, preferred_element_type=jnp.float32)
    key_float = key_heads.astype(jnp.float32)
    value_float = value_heads.astype(jnp.float32)
    inner_part = jnp.einsum("hts,shd->thd", scores * decay_mat, value_float, precision=HIGHEST)
    keep_mask = (doc_rows == doc_rows[-1]).astype(jnp.float32)
    tail_weight = jnp.exp(totals[:, None] - cumulative) * keep_mask[None, :]
    weighted_keys = key_float * jnp.transpose(tail_weight)[:, :, None]
    fresh_state = jnp.einsum("shd,she->hde", weighted_keys, value_float, precision=HIGHEST)
    carry_on = (doc_rows[-1] < first_place).astype(jnp.float32)
    factor = jnp.exp(totals) * carry_on
    read_mask = (doc_rows < first_place).astype(jnp.float32)[:, None] * jnp.transpose(
        jnp.exp(cumulative)
    )
    return (inner_part, fresh_state, factor, read_mask)


def combine_states(earlier, later_part):
    return (earlier[0] * later_part[0], later_part[0][:, None, None] * earlier[1] + later_part[1])


def lightning_part(query_lin, key_lin, value_lin, log_decay, doc_start):
    span_len = query_lin.shape[0]
    head_count = log_decay.shape[0]
    first_place = lax.axis_index("seq") * span_len
    query_heads = query_lin.reshape(span_len, head_count, DH)
    key_heads = key_lin.reshape(span_len, head_count, DH)
    value_heads = value_lin.reshape(span_len, head_count, DH)
    inner_part, fresh_state, factor, read_mask = span_terms(
        query_heads, key_heads, value_heads, log_decay, doc_start, first_place
    )
    identity = (jnp.ones((head_count,), jnp.float32), jnp.zeros((head_count, DH, DH), jnp.float32))
    unused, carried = prefix((factor, fresh_state), "seq", combine_states, identity)
    outer_part = (
        jnp.einsum("thd,hde->the", query_heads.astype(jnp.float32), carried, precision=HIGHEST)
        * read_mask[:, :, None]
    )
    mixed_out = inner_part + outer_part
    normed = mixed_out * lax.rsqrt(jnp.mean(mixed_out * mixed_out, axis=-1, keepdims=True) + 1e-06)
    return normed.astype(jnp.bfloat16).reshape(span_len, head_count * DH)


def softmax_part(query_soft, key_soft, value_soft, doc_start):
    queries, keys_local, values_local = (
        lax.all_to_all(query_soft, "head", split_axis=1, concat_axis=0, tiled=True),
        lax.all_to_all(key_soft, "head", split_axis=1, concat_axis=0, tiled=True),
        lax.all_to_all(value_soft, "head", split_axis=1, concat_axis=0, tiled=True),
    )
    span_len = queries.shape[0]
    kv_count = keys_local.shape[1] // DH
    group_size = queries.shape[1] // keys_local.shape[1]
    first_place = lax.axis_index("seq") * span_len
    query_places = first_place + jnp.arange(span_len, dtype=jnp.int32)
    query_heads = queries.reshape(span_len, kv_count, group_size, DH)
    score_scale = DH ** (-0.5)
    start_state = (
        jnp.full((span_len, kv_count, group_size), masked_score, jnp.float32),
        jnp.zeros((span_len, kv_count, group_size), jnp.float32),
        jnp.zeros((span_len, kv_count, group_size, DH), jnp.float32),
    )
    key_piece = lax.all_gather(keys_local, "seq", axis=0, tiled=True)
    value_piece = lax.all_gather(values_local, "seq", axis=0, tiled=True)
    piece_rows = key_piece.shape[0]
    block_rows = max(
        (divisor for divisor in range(1, min(piece_rows, 1024) + 1) if piece_rows % divisor == 0)
    )
    block_count = piece_rows // block_rows
    key_parts = key_piece.reshape(block_count, block_rows, kv_count, DH)
    value_parts = value_piece.reshape(block_count, block_rows, kv_count, DH)
    begin_rows = jnp.int32(0) + block_rows * jnp.arange(block_count, dtype=jnp.int32)

    def absorb_block(running, slices):
        key_block, value_block, begin_row = slices
        running_max, norm_sum, accum_out = running
        token_positions = begin_row + jnp.arange(block_rows, dtype=jnp.int32)
        allowed = (token_positions[None, :] <= query_places[:, None]) & (
            doc_start[:, None] <= token_positions[None, :]
        )
        allowed = allowed[:, None, None, :]
        scores = (
            jnp.einsum("tkgd,skd->tkgs", query_heads, key_block, preferred_element_type=jnp.float32)
            * score_scale
        )
        new_max = jnp.maximum(
            running_max, jnp.max(jnp.where(allowed, scores, masked_score), axis=-1)
        )
        raw_weight = jnp.where(allowed, jnp.exp(scores - new_max[..., None]), 0.0)
        shrink = jnp.exp(running_max - new_max)
        norm_sum = norm_sum * shrink + jnp.sum(raw_weight, axis=-1)
        accum_out = accum_out * shrink[..., None] + jnp.einsum(
            "tkgs,skd->tkgd",
            raw_weight.astype(jnp.bfloat16),
            value_block,
            preferred_element_type=jnp.float32,
        )
        running = (new_max, norm_sum, accum_out)
        return (running, None)

    final_state, unused = lax.scan(absorb_block, start_state, (key_parts, value_parts, begin_rows))
    running_max, norm_sum, accum_out = final_state
    soft_out = (
        (accum_out / norm_sum[..., None])
        .astype(jnp.bfloat16)
        .reshape(span_len, kv_count * group_size * DH)
    )
    soft_lse = jnp.transpose(
        (running_max + jnp.log(norm_sum)).reshape(span_len, kv_count * group_size)
    )
    return (soft_out, soft_lse)


def per_device(
    query_lin, key_lin, value_lin, log_decay, query_soft, key_soft, value_soft, doc_start
):
    lin_out = lightning_part(query_lin, key_lin, value_lin, log_decay, doc_start)
    soft_out, soft_lse = softmax_part(query_soft, key_soft, value_soft, doc_start)
    return (lin_out, soft_out, soft_lse)


def solution(mesh):
    return jax.shard_map(
        per_device,
        mesh=mesh,
        in_specs=(
            P("seq", "head"),
            P("seq", "head"),
            P("seq", "head"),
            P("head", "seq"),
            P(("seq", "head"), None),
            P(("seq", "head"), None),
            P(("seq", "head"), None),
            P("seq"),
        ),
        out_specs=(P("seq", "head"), P("seq", "head"), P("head", "seq")),
        check_vma=False,
    )
```

profile of v0, /device:TPU:0, one launch (start us, length us, event | category | flops | bytes accessed | tf_op | source)
XLA Modules:
  0.0 91.8 jit_solution(14963114871208304785)
XLA Ops:
  7.2 1.2 %slice.8 = s32[1]{0:T(128)} slice(s32[64]{0:T(128)} %param.17), slice={[63:64]} | slice | bytes 8 | tf_op jit(solution)/shard_map/slice | solution.py:48
  9.1 1.3 %compare_convert_fusion = (f32[64]{0:T(128)S(1)}, f32[64]{0:T(128)S(1)}) fusion(s32[64]{0:T(128)} %param.17, s32[]{:T(128)S(6)} %mul.138, s32[]{:T(128)} %bitcast.1), kind=kLoop, calls=%fused_computation.64 | loop fusion | flops 256 | bytes 776 | tf_op jit(solution)/shard_map/convert_element_type | solution.py:50
  10.4 0.9 reduce_window_sum.11
  11.6 2.4 %fusion.11 = f32[8,128,128]{2,1,0:T(8,128)} fusion(f32[64,8]{0,1:T(8,128)S(1)} %get-tuple-element.160, bf16[64,1024]{1,0:T(8,128)(2,1)S(1)} %copy-done, bf16[64,1024]{1,0:T(8,128)(2,1)} %param.11), kind=kOutput, calls=%fused_computation.22 | convolution fusion | flops 100794368 | bytes 788480 | tf_op jit(solution)/shard_map/shd,she->hde/dot_general | solution.py:47
  14.0 1.3 %copy_bitcast_fusion.4 = bf16[16,4,128]{2,0,1:T(8,128)(2,1)} fusion(bf16[16,512]{1,0:T(8,128)(2,1)} %param.15), kind=kLoop, calls=%fused_computation.50 | loop fusion | bytes 32768 | tf_op jit(solution)/shard_map/all_to_all | solution.py:84
  15.3 6.3 %all-to-all-start = ((bf16[16,4,128]{2,0,1:T(8,128)(2,1)}), bf16[16,4,128]{2,0,1:T(8,128)(2,1)S(1)}, u32[]{:S(2)}, u32[]{:S(2)}) async-start(bf16[16,4,128]{2,0,1:T(8,128)(2,1)} %copy_bitcast_fusion.4), calls=%async_computation | async-start | bytes 32768 | tf_op jit(solution)/shard_map/all_to_all | solution.py:84
  21.7 1.3 %copy_bitcast_fusion.3 = bf16[16,4,128]{2,0,1:T(8,128)(2,1)} fusion(bf16[16,512]{1,0:T(8,128)(2,1)} %param.16), kind=kLoop, calls=%fused_computation.49 | loop fusion | bytes 32768 | tf_op jit(solution)/shard_map/all_to_all | solution.py:85
  23.0 0.7 compare_and_fusion
  23.7 3.5 %all-to-all-done = bf16[16,4,128]{2,0,1:T(8,128)(2,1)S(1)} async-done(((bf16[16,4,128]{2,0,1:T(8,128)(2,1)}), bf16[16,4,128]{2,0,1:T(8,128)(2,1)S(1)}, u32[]{:S(2)}, u32[]{:S(2)}) %all-to-all-start) | async-done | bytes 16416 | tf_op jit(solution)/shard_map/all_to_all | solution.py:84
  27.3 3.3 %all-to-all-start.2 = ((bf16[16,4,128]{2,0,1:T(8,128)(2,1)}), bf16[16,4,128]{2,0,1:T(8,128)(2,1)S(1)}, u32[]{:S(2)}, u32[]{:S(2)}) async-start(bf16[16,4,128]{2,0,1:T(8,128)(2,1)} %copy_bitcast_fusion.3), calls=%async_computation.2 | async-start | bytes 32768 | tf_op jit(solution)/shard_map/all_to_all | solution.py:85
  30.5 1.2 %convolution_multiply_fusion.1 = f32[8,64,64]{2,1,0:T(8,128)S(1)} fusion(f32[8,64]{1,0:T(8,128)S(1)} %reduce_window_sum.11, pred[64,64]{1,0:T(8,128)(4,1)S(1)} %compare_and_fusion, bf16[64,1024]{1,0:T(8,128)(2,1)} %param.11, bf16[64,1024]{1,0:T(8,128)(2,1)} %param.10), kind=kOutput, calls=%fused_computation.10 | convolution fusion | flops 8519680 | bytes 399360 | tf_op jit(solution)/shard_map/thd,shd->hts/dot_general | solution.py:40
  31.7 1.2 %dynamic-slice = u32[1]{0:T(128)} dynamic-slice(u32[32]{0:T(128)} %constant.72, u32[]{:T(128)S(6)} %add.102), dynamic_slice_sizes={1} | dynamic-slice | bytes 12
  33.9 12.5 %all-reduce = f32[64]{0:T(128)S(1)} all-reduce(f32[64]{0:T(128)S(1)} %dynamic-update-slice), channel_id=2, replica_groups=mesh['seq'=8,'head'=4] {'seq'}, use_global_device_ids=true, to_apply=%add | all-reduce | flops 64 | bytes 512
  46.5 1.6 %copy.93 = bf16[2,4,8,1024]{3,2,0,1:T(8,128)(2,1)} copy(bf16[2,4,8,1024]{3,2,1,0:T(8,128)(2,1)} %bitcast.145) | data formatting | bytes 262144 | tf_op jit(solution)/shard_map/all_to_all | solution.py:83
  48.1 4.8 %all-to-all-start.1 = ((bf16[16,4,1024]{2,0,1:T(8,128)(2,1)}), bf16[16,4,1024]{2,0,1:T(8,128)(2,1)S(1)}, u32[]{:S(2)}, u32[]{:S(2)}) async-start(bf16[16,4,1024]{2,0,1:T(8,128)(2,1)} %bitcast.137), calls=%async_computation.1 | async-start | bytes 262144 | tf_op jit(solution)/shard_map/all_to_all | solution.py:83
  52.8 0.7 fusion.25
  53.6 9.1 %all_gather.19 = bf16[512,128]{1,0:T(8,128)(2,1)S(1)} all-gather(bf16[64,128]{1,0:T(8,128)(2,1)S(1)} %bitcast.148), channel_id=1, replica_groups=mesh['seq'=8,'head'=4] {'seq'}, dimensions={0}, use_global_device_ids=true | all-gather | bytes 147456 | tf_op jit(solution)/shard_map/all_gather | solution.py:99
  62.7 8.4 %all_gather.20 = bf16[512,128]{1,0:T(8,128)(2,1)S(1)} all-gather(bf16[64,128]{1,0:T(8,128)(2,1)S(1)} %bitcast.149), channel_id=1, replica_groups=mesh['seq'=8,'head'=4] {'seq'}, dimensions={0}, use_global_device_ids=true | all-gather | bytes 147456 | tf_op jit(solution)/shard_map/all_gather | solution.py:100
  71.1 0.4 select_reduce_fusion
  72.0 0.5 fusion.6
  72.5 0.7 copy.92
  73.1 0.6 fusion.33
  73.8 9.7 %while.9 = (s32[]{:T(128)}, f32[8,128,128]{2,1,0:T(8,128)S(1)}, s32[]{:T(128)}, f32[8,8]{1,0:T(8,128)S(1)}, f32[8,8,128,128]{3,2,1,0:T(8,128)}, /*index=5*/s32[]{:T(128)}, s32[]{:T(128)}) while((s32[]{:T(128)}, f32[8,128,128]{2,1,0:T(8,128)S(1)}, s32[]{:T(128)}, f32[8,8]{1,0:T(8,128)S(1)}, f32[8,8,128,128]{3,2,1,0:T(8,128)}, ...), condition=%wide.region_2.3_spmd.clone, body=%wide.region_1.2_spmd.clone.sunk | while | flops 524292 | bytes 1573065 | solution.py:27
  73.8 1.2 %fusion.49 = f32[8,128,128]{2,1,0:T(8,128)S(1)} fusion(f32[8,8,128,128]{3,2,1,0:T(8,128)} %get-tuple-element.216, s32[]{:T(128)} %get-tuple-element.205, f32[8,128,128]{2,1,0:T(8,128)S(1)} %get-tuple-element.206, f32[8]{0:T(128)S(1)} %dynamic-slice_bitcast_fusion.2, pred[]{:T(512)S(6)} %compare.3, pred[]{:T(512)S(6)} %lt.33), kind=kLoop, calls=%fused_computation.1.clone.1 | loop fusion | flops 524288 | bytes 1572902 | tf_op jit(solution)/shard_map/while/body/eval_jaxpr/jit(_where)/select_n | solution.py:25
  75.0 1.2 %fusion.49 = f32[8,128,128]{2,1,0:T(8,128)S(1)} fusion(f32[8,8,128,128]{3,2,1,0:T(8,128)} %get-tuple-element.216, s32[]{:T(128)} %get-tuple-element.205, f32[8,128,128]{2,1,0:T(8,128)S(1)} %get-tuple-element.206, f32[8]{0:T(128)S(1)} %dynamic-slice_bitcast_fusion.2, pred[]{:T(512)S(6)} %compare.3, pred[]{:T(512)S(6)} %lt.33), kind=kLoop, calls=%fused_computation.1.clone.1 | loop fusion | flops 524288 | bytes 1572902 | tf_op jit(solution)/shard_map/while/body/eval_jaxpr/jit(_where)/select_n | solution.py:25
  76.2 1.2 %fusion.49 = f32[8,128,128]{2,1,0:T(8,128)S(1)} fusion(f32[8,8,128,128]{3,2,1,0:T(8,128)} %get-tuple-element.216, s32[]{:T(128)} %get-tuple-element.205, f32[8,128,128]{2,1,0:T(8,128)S(1)} %get-tuple-element.206, f32[8]{0:T(128)S(1)} %dynamic-slice_bitcast_fusion.2, pred[]{:T(512)S(6)} %compare.3, pred[]{:T(512)S(6)} %lt.33), kind=kLoop, calls=%fused_computation.1.clone.1 | loop fusion | flops 524288 | bytes 1572902 | tf_op jit(solution)/shard_map/while/body/eval_jaxpr/jit(_where)/select_n | solution.py:25
  77.4 1.2 %fusion.49 = f32[8,128,128]{2,1,0:T(8,128)S(1)} fusion(f32[8,8,128,128]{3,2,1,0:T(8,128)} %get-tuple-element.216, s32[]{:T(128)} %get-tuple-element.205, f32[8,128,128]{2,1,0:T(8,128)S(1)} %get-tuple-element.206, f32[8]{0:T(128)S(1)} %dynamic-slice_bitcast_fusion.2, pred[]{:T(512)S(6)} %compare.3, pred[]{:T(512)S(6)} %lt.33), kind=kLoop, calls=%fused_computation.1.clone.1 | loop fusion | flops 524288 | bytes 1572902 | tf_op jit(solution)/shard_map/while/body/eval_jaxpr/jit(_where)/select_n | solution.py:25
  78.6 1.2 %fusion.49 = f32[8,128,128]{2,1,0:T(8,128)S(1)} fusion(f32[8,8,128,128]{3,2,1,0:T(8,128)} %get-tuple-element.216, s32[]{:T(128)} %get-tuple-element.205, f32[8,128,128]{2,1,0:T(8,128)S(1)} %get-tuple-element.206, f32[8]{0:T(128)S(1)} %dynamic-slice_bitcast_fusion.2, pred[]{:T(512)S(6)} %compare.3, pred[]{:T(512)S(6)} %lt.33), kind=kLoop, calls=%fused_computation.1.clone.1 | loop fusion | flops 524288 | bytes 1572902 | tf_op jit(solution)/shard_map/while/body/eval_jaxpr/jit(_where)/select_n | solution.py:25
  79.8 1.2 %fusion.49 = f32[8,128,128]{2,1,0:T(8,128)S(1)} fusion(f32[8,8,128,128]{3,2,1,0:T(8,128)} %get-tuple-element.216, s32[]{:T(128)} %get-tuple-element.205, f32[8,128,128]{2,1,0:T(8,128)S(1)} %get-tuple-element.206, f32[8]{0:T(128)S(1)} %dynamic-slice_bitcast_fusion.2, pred[]{:T(512)S(6)} %compare.3, pred[]{:T(512)S(6)} %lt.33), kind=kLoop, calls=%fused_computation.1.clone.1 | loop fusion | flops 524288 | bytes 1572902 | tf_op jit(solution)/shard_map/while/body/eval_jaxpr/jit(_where)/select_n | solution.py:25
  81.0 1.2 %fusion.49 = f32[8,128,128]{2,1,0:T(8,128)S(1)} fusion(f32[8,8,128,128]{3,2,1,0:T(8,128)} %get-tuple-element.216, s32[]{:T(128)} %get-tuple-element.205, f32[8,128,128]{2,1,0:T(8,128)S(1)} %get-tuple-element.206, f32[8]{0:T(128)S(1)} %dynamic-slice_bitcast_fusion.2, pred[]{:T(512)S(6)} %compare.3, pred[]{:T(512)S(6)} %lt.33), kind=kLoop, calls=%fused_computation.1.clone.1 | loop fusion | flops 524288 | bytes 1572902 | tf_op jit(solution)/shard_map/while/body/eval_jaxpr/jit(_where)/select_n | solution.py:25
  82.2 1.2 %fusion.49 = f32[8,128,128]{2,1,0:T(8,128)S(1)} fusion(f32[8,8,128,128]{3,2,1,0:T(8,128)} %get-tuple-element.216, s32[]{:T(128)} %get-tuple-element.205, f32[8,128,128]{2,1,0:T(8,128)S(1)} %get-tuple-element.206, f32[8]{0:T(128)S(1)} %dynamic-slice_bitcast_fusion.2, pred[]{:T(512)S(6)} %compare.3, pred[]{:T(512)S(6)} %lt.33), kind=kLoop, calls=%fused_computation.1.clone.1 | loop fusion | flops 524288 | bytes 1572902 | tf_op jit(solution)/shard_map/while/body/eval_jaxpr/jit(_where)/select_n | solution.py:25
  84.2 0.8 copy_bitcast_fusion.1
  (33 shorter events, 2.0 us)
Async XLA Ops:
  7.2 4.4 %copy-start = (bf16[64,1024]{1,0:T(8,128)(2,1)S(1)}, bf16[64,1024]{1,0:T(8,128)(2,1)}, u32[]{:S(2)}) copy-start(bf16[64,1024]{1,0:T(8,128)(2,1)} %param.12) | copy-start | bytes 393220
  7.2 66.6 %all-gather.4.cloned.1.call-start = ((), (), s32[]{:S(2)}) async-start(), calls=%async_computation.3 | async-start | bytes 4718592 | tf_op jit(solution)/shard_map/all_gather | solution.py:15
  15.3 11.9 %all-to-all-start = ((bf16[16,4,128]{2,0,1:T(8,128)(2,1)}), bf16[16,4,128]{2,0,1:T(8,128)(2,1)S(1)}, u32[]{:S(2)}, u32[]{:S(2)}) async-start(bf16[16,4,128]{2,0,1:T(8,128)(2,1)} %copy_bitcast_fusion.4), calls=%async_computation | async-start | bytes 32768 | tf_op jit(solution)/shard_map/all_to_all | solution.py:84
  27.3 20.8 %all-to-all-start.2 = ((bf16[16,4,128]{2,0,1:T(8,128)(2,1)}), bf16[16,4,128]{2,0,1:T(8,128)(2,1)S(1)}, u32[]{:S(2)}, u32[]{:S(2)}) async-start(bf16[16,4,128]{2,0,1:T(8,128)(2,1)} %copy_bitcast_fusion.3), calls=%async_computation.2 | async-start | bytes 32768 | tf_op jit(solution)/shard_map/all_to_all | solution.py:85
  48.1 23.0 %all-to-all-start.1 = ((bf16[16,4,1024]{2,0,1:T(8,128)(2,1)}), bf16[16,4,1024]{2,0,1:T(8,128)(2,1)S(1)}, u32[]{:S(2)}, u32[]{:S(2)}) async-start(bf16[16,4,1024]{2,0,1:T(8,128)(2,1)} %bitcast.137), calls=%async_computation.1 | async-start | bytes 262144 | tf_op jit(solution)/shard_map/all_to_all | solution.py:83
  72.5 11.0 %copy-start.1 = (bf16[64,1024]{1,0:T(8,128)(2,1)S(1)}, bf16[64,1024]{1,0:T(8,128)(2,1)}, u32[]{:S(2)}) copy-start(bf16[64,1024]{1,0:T(8,128)(2,1)} %param.10) | copy-start | bytes 393220
Sparse Core Ops, SparseCore 0:
  14.1 39.5 all-gather.3
where the time goes:
time: 92.9 us; the launch traced here: 91.8 us
  blocking collectives  30 us (32%)
  between operations  15.5 us (17%)
  other arithmetic  15.1 us (16%)
  starting transfers between devices  14.4 us (16%)
  local copies, waits for them, and re-layouts  7.97 us (9%)
  matrix products  5.12 us (6%)
  waiting for transfers between devices  3.56 us (4%)
    unnamed x1, blocking collectives  12.5 us
    select_n x8, other arithmetic, lap(): return jax.tree.map(lambda a, b: jnp.where(reached, a, b), new, before)  9.38 us
    all_gather x1, blocking collectives, softmax_part(): key_piece = lax.all_gather(keys_local, 'seq', axis=0, tiled=True)  9.07 us
    all_gather x1, blocking collectives, softmax_part(): value_piece = lax.all_gather(values_local, 'seq', axis=0, tiled=True)  8.36 us
    all_to_all x1, starting transfers between devices, softmax_part(): lax.all_to_all(key_soft, 'head', split_axis=1, concat_axis=0, tiled=True)  6.32 us
    all_to_all x1, starting transfers between devices, softmax_part(): lax.all_to_all(query_soft, 'head', split_axis=1, concat_axis=0, tiled=True)  4.78 us
    all_to_all x1, waiting for transfers between devices, softmax_part(): lax.all_to_all(key_soft, 'head', split_axis=1, concat_axis=0, tiled=True)  3.54 us
    all_to_all x1, starting transfers between devices, softmax_part(): lax.all_to_all(value_soft, 'head', split_axis=1, concat_axis=0, tiled=True)  3.25 us
  transfers between devices with their start and end apart: 4, of which 1 were waited for; matrix products, arithmetic and copies ran while one was open for 12% of the time, Pallas kernels for 0%

commit v1 on v0

--- a/solution.py
+++ b/solution.py
@@ -1,7 +1,12 @@
+import functools
+
 import jax
 import jax.numpy as jnp
 from jax import lax
+from jax.experimental import pallas as pl
+from jax.experimental.pallas import tpu as pltpu
 from jax.sharding import PartitionSpec as P
+
 
 DH = 128
 
@@ -147,9 +152,271 @@
     return (soft_out, soft_lse)
 
 
+MESH = pl.DeviceIdType.MESH
+NT = (((1,), (1,)), ((), ()))
+
+
+def fused_kernel(
+    n, m, q_in, k_in, v_in, ld_in, qs_in, ks_in, vs_in, doc_in,
+    lin_out, soft_out, lse_out,
+    stage, lin_all, aux, aux_all, ld_v, doc_v, qs, kv, lin_v, soft_v, lse_v, bias,
+    loc_sem, lin_s, lin_r, aux_s, aux_r, kv1_s, kv1_r, qs_s, qs_r, kv2_s, kv2_r, out_s, out_r,
+):
+    span, heads = doc_in.shape[1], ld_in.shape[0]
+    rows = qs_in.shape[0]
+    tokens = n * span
+    me, hd = lax.axis_index("seq"), lax.axis_index("head")
+
+    barrier = pltpu.get_barrier_semaphore()
+    seq_peers = [lax.rem(me + j, n) for j in range(1, n)]
+    head_peers = [lax.rem(hd + j, m) for j in range(1, m)]
+    for peer in seq_peers:
+        pl.semaphore_signal(barrier, inc=1, device_id={"seq": peer}, device_id_type=MESH)
+    for peer in head_peers:
+        pl.semaphore_signal(barrier, inc=1, device_id={"head": peer}, device_id_type=MESH)
+
+    def cols(index, width=DH):
+        return pl.ds(pl.multiple_of(index * width, width), width)
+
+    def own_rows(index, count):
+        return pl.ds(pl.multiple_of(index * count, count), count)
+
+    loads = [
+        pltpu.make_async_copy(ld_in, ld_v, loc_sem.at[0]),
+        pltpu.make_async_copy(doc_in, doc_v, loc_sem.at[1]),
+        pltpu.make_async_copy(q_in, stage.at[0], loc_sem.at[2]),
+        pltpu.make_async_copy(k_in, stage.at[1], loc_sem.at[3]),
+        pltpu.make_async_copy(v_in, stage.at[2], loc_sem.at[4]),
+        pltpu.make_async_copy(
+            ks_in.at[:, cols(hd)], kv.at[0, own_rows(me * m + hd, rows), :], loc_sem.at[5]
+        ),
+        pltpu.make_async_copy(
+            vs_in.at[:, cols(hd)], kv.at[1, own_rows(me * m + hd, rows), :], loc_sem.at[6]
+        ),
+        pltpu.make_async_copy(
+            qs_in.at[:, cols(hd, heads * DH)], qs.at[own_rows(hd, rows), :], loc_sem.at[7]
+        ),
+    ]
+    for load in loads:
+        load.start()
+    aux[...] = jnp.zeros_like(aux)
+    loads[0].wait()
+    loads[1].wait()
+    aux[0:heads, 0:span] = ld_v[...]
+    aux[heads : heads + 1, 0:span] = doc_v[...].astype(jnp.float32)
+    aux_all[me] = aux[...]
+    for load in loads[2:5]:
+        load.wait()
+    own = pltpu.make_async_copy(
+        stage.at[:, :, cols(me)], lin_all.at[:, own_rows(me, span), :], loc_sem.at[8]
+    )
+    own.start()
+    pl.semaphore_wait(barrier, n + m - 2)
+
+    def remote(src, dst, send, recv, device):
+        return pltpu.make_async_remote_copy(
+            src_ref=src, dst_ref=dst, send_sem=send, recv_sem=recv,
+            device_id=device, device_id_type=MESH,
+        )
+
+    kv1, qsc = [], []
+    for j, peer in enumerate(head_peers):
+        dst_rows = own_rows(me * m + hd, rows)
+        for side, src in enumerate((ks_in, vs_in)):
+            kv1.append(
+                remote(
+                    src.at[:, cols(peer)], kv.at[side, dst_rows, :],
+                    kv1_s.at[2 * j + side], kv1_r.at[2 * j + side], {"head": peer},
+                )
+            )
+        qsc.append(
+            remote(
+                qs_in.at[:, cols(peer, heads * DH)], qs.at[own_rows(hd, rows), :],
+                qs_s.at[j], qs_r.at[j], {"head": peer},
+            )
+        )
+    auxc = [
+        remote(aux, aux_all.at[me], aux_s.at[j], aux_r.at[j], {"seq": peer})
+        for j, peer in enumerate(seq_peers)
+    ]
+    linc = [
+        remote(
+            stage.at[:, :, cols(peer)], lin_all.at[:, own_rows(me, span), :],
+            lin_s.at[j], lin_r.at[j], {"seq": peer},
+        )
+        for j, peer in enumerate(seq_peers)
+    ]
+    mine = kv.at[:, own_rows(me, span), :]
+    kv2 = [
+        remote(mine, mine, kv2_s.at[j], kv2_r.at[j], {"seq": peer})
+        for j, peer in enumerate(seq_peers)
+    ]
+    outc = [
+        remote(
+            lin_v.at[own_rows(peer, span), :], lin_out.at[:, cols(me)],
+            out_s.at[j], out_r.at[j], {"seq": peer},
+        )
+        for j, peer in enumerate(seq_peers)
+    ]
+    for copy in kv1 + auxc + linc + qsc:
+        copy.start()
+    loads[5].wait()
+    loads[6].wait()
+    for copy in kv1:
+        copy.wait_recv()
+    for copy in kv2:
+        copy.start()
+
+    def iota(shape, dim):
+        return lax.broadcasted_iota(jnp.int32, shape, dim)
+
+    eye_s = iota((span, span), 0) == iota((span, span), 1)
+    doc_col = jnp.sum(jnp.where(eye_s, doc_v[...].astype(jnp.float32), 0.0), axis=1, keepdims=True)
+    place = me * span + iota((span, tokens), 0)
+    key_at = iota((span, tokens), 1)
+    open_s = (key_at <= place) & (key_at >= doc_col.astype(jnp.int32))
+    half = jnp.where(open_s, 0.0, masked_score)
+    bias[0:span, :] = half
+    bias[span : 2 * span, :] = half
+
+    for copy in auxc:
+        copy.wait_recv()
+    blk = 2 * span
+    eye = iota((blk, blk), 0) == iota((blk, blk), 1)
+    tri = iota((blk, blk), 0) >= iota((blk, blk), 1)
+    sum_col, sum_row, doc_cols = [], [], []
+    before = jnp.zeros((1, 1), jnp.float32)
+    for i in range(tokens // blk):
+        decay = jnp.concatenate(
+            [aux_all[2 * i + b, pl.ds(me, 1), 0:span] for b in range(2)], axis=1
+        )
+        docs = jnp.concatenate(
+            [aux_all[2 * i + b, heads : heads + 1, 0:span] for b in range(2)], axis=1
+        )
+        column = jnp.sum(jnp.where(tri, decay, 0.0), axis=1, keepdims=True) + before
+        before = before + jnp.sum(decay, axis=1, keepdims=True)
+        sum_col.append(column)
+        sum_row.append(jnp.sum(jnp.where(eye, column, 0.0), axis=0, keepdims=True))
+        doc_cols.append(jnp.sum(jnp.where(eye, docs, 0.0), axis=1, keepdims=True).astype(jnp.int32))
+
+    own.wait()
+    for copy in linc:
+        copy.wait_recv()
+    for i in range(tokens // blk):
+        here = slice(i * blk, (i + 1) * blk)
+        reach = (i + 1) * blk
+        score = lax.dot_general(
+            lin_all[0, here, :], lin_all[1, 0:reach, :], NT, preferred_element_type=jnp.float32
+        )
+        gap = sum_col[i] - jnp.concatenate(sum_row[: i + 1], axis=1)
+        at = iota((blk, reach), 1)
+        is_open = (at >= doc_cols[i]) & (at <= i * blk + iota((blk, reach), 0))
+        mix = jnp.where(is_open, score * jnp.exp(gap), 0.0)
+        out = jnp.dot(
+            mix.astype(jnp.bfloat16), lin_all[2, 0:reach, :], preferred_element_type=jnp.float32
+        )
+        normed = out * lax.rsqrt(jnp.mean(out * out, axis=1, keepdims=True) + 1e-06)
+        lin_v[here, :] = normed.astype(jnp.bfloat16)
+    for copy in outc:
+        copy.start()
+    own_out = pltpu.make_async_copy(
+        lin_v.at[own_rows(me, span), :], lin_out.at[:, cols(me)], loc_sem.at[9]
+    )
+    own_out.start()
+
+    loads[7].wait()
+    for copy in qsc + kv2:
+        copy.wait_recv()
+    stores = []
+    for i in range(heads // 2):
+        queries = jnp.concatenate(
+            [qs[:, g * DH : (g + 1) * DH] for g in (2 * i, 2 * i + 1)], axis=0
+        )
+        score = lax.dot_general(queries, kv[0], NT, preferred_element_type=jnp.float32)
+        score = score * DH ** (-0.5) + bias[...]
+        top = jnp.max(score, axis=1, keepdims=True)
+        weight = jnp.exp(score - top)
+        total = jnp.sum(weight, axis=1, keepdims=True)
+        out = jnp.dot(weight.astype(jnp.bfloat16), kv[1], preferred_element_type=jnp.float32)
+        out = (out / total).astype(jnp.bfloat16)
+        lse = top + jnp.log(total)
+        for b in range(2):
+            g = 2 * i + b
+            part = slice(b * span, (b + 1) * span)
+            soft_v[:, g * DH : (g + 1) * DH] = out[part]
+            lse_v[g : g + 1, :] = jnp.sum(
+                jnp.where(eye_s, lse[part], 0.0), axis=0, keepdims=True
+            )
+        pair = slice(2 * i * DH, 2 * (i + 1) * DH)
+        stores.append(
+            pltpu.make_async_copy(soft_v.at[:, pair], soft_out.at[:, pair], loc_sem.at[10 + i])
+        )
+        stores[-1].start()
+    stores.append(pltpu.make_async_copy(lse_v, lse_out, loc_sem.at[10 + heads // 2]))
+    stores[-1].start()
+
+    for copy in outc:
+        copy.wait_recv()
+    own_out.wait()
+    for copy in stores:
+        copy.wait()
+    for copy in kv1 + auxc + linc + qsc + kv2 + outc:
+        copy.wait_send()
+
+
+def fused(n, m, query_lin, key_lin, value_lin, log_decay, query_soft, key_soft, value_soft, doc_start):
+    span, heads = query_lin.shape[0], log_decay.shape[0]
+    tokens, rows = n * span, query_soft.shape[0]
+    bf16, f32 = jnp.bfloat16, jnp.float32
+    any_spec = pl.BlockSpec(memory_space=pl.ANY)
+    dma = pltpu.SemaphoreType.DMA
+    return pl.pallas_call(
+        functools.partial(fused_kernel, n, m),
+        out_shape=(
+            jax.ShapeDtypeStruct((span, heads * DH), bf16),
+            jax.ShapeDtypeStruct((span, heads * DH), bf16),
+            jax.ShapeDtypeStruct((heads, span), f32),
+        ),
+        in_specs=[any_spec] * 8,
+        out_specs=(any_spec,) * 3,
+        scratch_shapes=[
+            pltpu.VMEM((3, span, heads * DH), bf16),
+            pltpu.VMEM((3, tokens, DH), bf16),
+            pltpu.VMEM((2 * heads, DH), f32),
+            pltpu.VMEM((n, 2 * heads, DH), f32),
+            pltpu.VMEM((heads, span), f32),
+            pltpu.VMEM((1, span), jnp.int32),
+            pltpu.VMEM((span, heads * DH), bf16),
+            pltpu.VMEM((2, tokens, DH), bf16),
+            pltpu.VMEM((tokens, DH), bf16),
+            pltpu.VMEM((span, heads * DH), bf16),
+            pltpu.VMEM((heads, span), f32),
+            pltpu.VMEM((2 * span, tokens), f32),
+            dma((11 + heads // 2,)),
+        ]
+        + [dma((n - 1,))] * 4
+        + [dma((2 * (m - 1),))] * 2
+        + [dma((m - 1,))] * 2
+        + [dma((n - 1,))] * 4,
+        compiler_params=pltpu.CompilerParams(
+            collective_id=0, has_side_effects=True, vmem_limit_bytes=32 * 1024 * 1024
+        ),
+    )(
+        query_lin, key_lin, value_lin, log_decay, query_soft, key_soft, value_soft,
+        doc_start.reshape(1, span),
+    )
+
+
 def per_device(
     query_lin, key_lin, value_lin, log_decay, query_soft, key_soft, value_soft, doc_start
 ):
+    n, m = lax.axis_size("seq"), lax.axis_size("head")
+    span, heads = query_lin.shape[0], log_decay.shape[0]
+    if heads == n and span == DH // 2 and key_soft.shape[1] == m * DH and n % 2 == 0:
+        return fused(
+            n, m, query_lin, key_lin, value_lin, log_decay,
+            query_soft, key_soft, value_soft, doc_start,
+        )
     lin_out = lightning_part(query_lin, key_lin, value_lin, log_decay, doc_start)
     soft_out, soft_lse = softmax_part(query_soft, key_soft, value_soft, doc_start)
     return (lin_out, soft_out, soft_lse)

time: 92.9 us -> 27.3 us (0.29)
  blocking collectives: 30 us -> 0 us
  Pallas kernels: 0 us -> 17.9 us
  other arithmetic: 15.1 us -> 0 us
  between operations: 15.5 us -> 0.66 us
  starting transfers between devices: 14.4 us -> 0 us
  matrix products: 5.12 us -> 0 us
  waiting for transfers between devices: 3.56 us -> 0 us
    pallas_call x0 -> x1, Pallas kernels: none -> 17.9 us  [fused(): pl.pallas_call(functools.partial(fused_kernel, n, m), out_shape=(jax.Shap...]
    all_gather x2 -> x0, blocking collectives: 17.4 us -> none  [the longest x1 9.07 us: softmax_part(): key_piece = lax.all_gather(keys_local, 'seq', axis=0, tiled=True)]
    all_to_all x3 -> x0, starting transfers between devices: 14.4 us -> none  [the longest x1 6.32 us: softmax_part(): lax.all_to_all(key_soft, 'head', split_axis=1, concat_axis=0, tiled=True)]
    unnamed x1 -> x0, blocking collectives: 12.5 us -> none
    select_n x8 -> x0, other arithmetic: 9.38 us -> none  [lap(): return jax.tree.map(lambda a, b: jnp.where(reached, a, b), new, before)]
    unnamed x9 -> x19, local copies, waits for them, and re-layouts: 2.2 us -> 8.29 us
    dot_general x6 -> x0, matrix products: 5.12 us -> none  [the longest x1 2.39 us: span_terms(): jnp.einsum('shd,she->hde', weighted_keys, value_float, precision=HIGHEST)]
    all_to_all x3 -> x0, local copies, waits for them, and re-layouts: 4.22 us -> none  [the longest x1 1.57 us: softmax_part(): lax.all_to_all(query_soft, 'head', split_axis=1, concat_axis=0, tiled=True)]
  transfers between devices with their start and end apart: 4 -> 0, of which waited for: 1 -> 0; matrix products, arithmetic and copies ran while one was open for 12% -> 0% of each run, Pallas kernels for 0% -> 0%
where the time goes in v1:
time: 27.3 us; the launch traced here: 26.9 us
  Pallas kernels  17.9 us (66%)
  local copies, waits for them, and re-layouts  8.29 us (30%)
  between operations  0.66 us (2%)
    pallas_call x1, Pallas kernels, fused(): pl.pallas_call(functools.partial(fused_kernel, n, m), out_shape=(jax.Shap...  17.9 us
    unnamed x19, local copies, waits for them, and re-layouts  8.29 us

profile of v1, /device:TPU:0, one launch (start us, length us, event | category | flops | bytes accessed | tf_op | source)
XLA Modules:
  0.0 26.9 jit_solution(1679560738333278158)
XLA Ops:
  0.6 0.0 copy-start.7
  0.6 0.6 %copy-done.7 = s32[64]{0:T(128)S(1)} copy-done((s32[64]{0:T(128)S(1)}, s32[64]{0:T(128)}, u32[]{:S(2)}) %copy-start.7) | copy-done | bytes 280
  1.3 0.0 copy-start
  1.3 0.9 %copy-done = bf16[64,1024]{1,0:T(8,128)(2,1)S(1)} copy-done((bf16[64,1024]{1,0:T(8,128)(2,1)S(1)}, bf16[64,1024]{1,0:T(8,128)(2,1)}, u32[]{:S(2)}) %copy-start) | copy-done | bytes 131096
  2.2 0.0 copy-start.1
  2.2 0.9 %copy-done.1 = bf16[64,1024]{1,0:T(8,128)(2,1)S(1)} copy-done((bf16[64,1024]{1,0:T(8,128)(2,1)S(1)}, bf16[64,1024]{1,0:T(8,128)(2,1)}, u32[]{:S(2)}) %copy-start.1) | copy-done | bytes 131096
  3.1 0.0 copy-start.2
  3.1 0.9 %copy-done.2 = bf16[64,1024]{1,0:T(8,128)(2,1)S(1)} copy-done((bf16[64,1024]{1,0:T(8,128)(2,1)S(1)}, bf16[64,1024]{1,0:T(8,128)(2,1)}, u32[]{:S(2)}) %copy-start.2) | copy-done | bytes 131096
  4.0 0.0 copy-start.3
  4.0 0.9 %copy-done.3 = bf16[16,4096]{1,0:T(8,128)(2,1)S(1)} copy-done((bf16[16,4096]{1,0:T(8,128)(2,1)S(1)}, bf16[16,4096]{1,0:T(8,128)(2,1)}, u32[]{:S(2)}) %copy-start.3) | copy-done | bytes 131096
  4.9 0.0 copy-start.4
  4.9 0.7 %copy-done.4 = bf16[16,512]{1,0:T(8,128)(2,1)S(1)} copy-done((bf16[16,512]{1,0:T(8,128)(2,1)S(1)}, bf16[16,512]{1,0:T(8,128)(2,1)}, u32[]{:S(2)}) %copy-start.4) | copy-done | bytes 16408
  5.6 0.0 copy-start.5
  5.6 0.7 %copy-done.5 = bf16[16,512]{1,0:T(8,128)(2,1)S(1)} copy-done((bf16[16,512]{1,0:T(8,128)(2,1)S(1)}, bf16[16,512]{1,0:T(8,128)(2,1)}, u32[]{:S(2)}) %copy-start.5) | copy-done | bytes 16408
  6.3 0.0 copy-start.6
  6.3 0.7 %copy-done.6 = f32[8,64]{1,0:T(8,128)S(1)} copy-done((f32[8,64]{1,0:T(8,128)S(1)}, f32[8,64]{1,0:T(8,128)}, u32[]{:S(2)}) %copy-start.6) | copy-done | bytes 2072
  7.0 17.9 %shard_map.103 = (bf16[64,1024]{1,0:T(8,128)(2,1)S(1)}, bf16[64,1024]{1,0:T(8,128)(2,1)S(1)}, f32[8,64]{1,0:T(8,128)S(1)}) custom-call(bf16[64,1024]{1,0:T(8,128)(2,1)S(1)} %copy-done, bf16[64,1024]{1,0:T(8,128)(2,1)S(1)} %copy-done.1, bf16[64,1024]{1,0:T(8,128)(2,1)S(1)} %copy-done.2, f32[8,64]{1,0:T(8,128)S(1)} %copy-done.6, ...), custom_call_target="tpu_custom_call" | custom-call | tf_op jit(solution)/shard_map/pallas_call | solution.py:373
  25.0 0.7 %copy.14 = bf16[64,1024]{1,0:T(8,128)(2,1)} copy(bf16[64,1024]{1,0:T(8,128)(2,1)S(1)} %get-tuple-element.6) | data formatting | bytes 262144
  25.6 0.7 %copy.15 = bf16[64,1024]{1,0:T(8,128)(2,1)} copy(bf16[64,1024]{1,0:T(8,128)(2,1)S(1)} %get-tuple-element.7) | data formatting | bytes 262144
  26.3 0.6 %copy.16 = f32[8,64]{1,0:T(8,128)} copy(f32[8,64]{1,0:T(8,128)S(1)} %get-tuple-element.8) | data formatting | bytes 4096
Async XLA Ops:
  0.6 0.7 %copy-start.7 = (s32[64]{0:T(128)S(1)}, s32[64]{0:T(128)}, u32[]{:S(2)}) copy-start(s32[64]{0:T(128)} %param.15) | copy-start | bytes 772
  1.3 0.9 %copy-start = (bf16[64,1024]{1,0:T(8,128)(2,1)S(1)}, bf16[64,1024]{1,0:T(8,128)(2,1)}, u32[]{:S(2)}) copy-start(bf16[64,1024]{1,0:T(8,128)(2,1)} %q_in.1) | copy-start | bytes 393220
  2.2 0.9 %copy-start.1 = (bf16[64,1024]{1,0:T(8,128)(2,1)S(1)}, bf16[64,1024]{1,0:T(8,128)(2,1)}, u32[]{:S(2)}) copy-start(bf16[64,1024]{1,0:T(8,128)(2,1)} %k_in.1) | copy-start | bytes 393220
  3.1 0.9 %copy-start.2 = (bf16[64,1024]{1,0:T(8,128)(2,1)S(1)}, bf16[64,1024]{1,0:T(8,128)(2,1)}, u32[]{:S(2)}) copy-start(bf16[64,1024]{1,0:T(8,128)(2,1)} %v_in.1) | copy-start | bytes 393220
  4.0 0.9 %copy-start.3 = (bf16[16,4096]{1,0:T(8,128)(2,1)S(1)}, bf16[16,4096]{1,0:T(8,128)(2,1)}, u32[]{:S(2)}) copy-start(bf16[16,4096]{1,0:T(8,128)(2,1)} %qs_in.1) | copy-start | bytes 393220
  4.9 0.7 %copy-start.4 = (bf16[16,512]{1,0:T(8,128)(2,1)S(1)}, bf16[16,512]{1,0:T(8,128)(2,1)}, u32[]{:S(2)}) copy-start(bf16[16,512]{1,0:T(8,128)(2,1)} %ks_in.1) | copy-start | bytes 49156
  5.6 0.7 %copy-start.5 = (bf16[16,512]{1,0:T(8,128)(2,1)S(1)}, bf16[16,512]{1,0:T(8,128)(2,1)}, u32[]{:S(2)}) copy-start(bf16[16,512]{1,0:T(8,128)(2,1)} %vs_in.1) | copy-start | bytes 49156
  6.3 0.7 %copy-start.6 = (f32[8,64]{1,0:T(8,128)S(1)}, f32[8,64]{1,0:T(8,128)}, u32[]{:S(2)}) copy-start(f32[8,64]{1,0:T(8,128)} %ld_in.1) | copy-start | bytes 6148

commit v2 on v1

--- a/solution.py
+++ b/solution.py
@@ -312,8 +312,11 @@
         at = iota((blk, reach), 1)
         is_open = (at >= doc_cols[i]) & (at <= i * blk + iota((blk, reach), 0))
         mix = jnp.where(is_open, score * jnp.exp(gap), 0.0)
-        out = jnp.dot(
-            mix.astype(jnp.bfloat16), lin_all[2, 0:reach, :], preferred_element_type=jnp.float32
+        high = mix.astype(jnp.bfloat16)
+        low = (mix - high.astype(jnp.float32)).astype(jnp.bfloat16)
+        values = lin_all[2, 0:reach, :]
+        out = jnp.dot(high, values, preferred_element_type=jnp.float32) + jnp.dot(
+            low, values, preferred_element_type=jnp.float32
         )
         normed = out * lax.rsqrt(jnp.mean(out * out, axis=1, keepdims=True) + 1e-06)
         lin_v[here, :] = normed.astype(jnp.bfloat16)
@@ -369,8 +372,9 @@
     tokens, rows = n * span, query_soft.shape[0]
     bf16, f32 = jnp.bfloat16, jnp.float32
     any_spec = pl.BlockSpec(memory_space=pl.ANY)
+    hbm_spec = pl.BlockSpec(memory_space=pltpu.HBM)
     dma = pltpu.SemaphoreType.DMA
-    return pl.pallas_call(
+    results = pl.pallas_call(
         functools.partial(fused_kernel, n, m),
         out_shape=(
             jax.ShapeDtypeStruct((span, heads * DH), bf16),
@@ -401,10 +405,28 @@
         compiler_params=pltpu.CompilerParams(
             collective_id=0, has_side_effects=True, vmem_limit_bytes=32 * 1024 * 1024
         ),
-    )(
+    )(*(pltpu.with_memory_space_constraint(x, pltpu.HBM) for x in (
         query_lin, key_lin, value_lin, log_decay, query_soft, key_soft, value_soft,
         doc_start.reshape(1, span),
-    )
+    )))
+    return pl.pallas_call(
+        store_kernel,
+        out_shape=tuple(jax.ShapeDtypeStruct(part.shape, part.dtype) for part in results),
+        in_specs=[any_spec] * 3,
+        out_specs=(hbm_spec,) * 3,
+        scratch_shapes=[dma((3,))],
+    )(*(pltpu.with_memory_space_constraint(part, pltpu.VMEM) for part in results))
+
+
+def store_kernel(a, b, c, a_out, b_out, c_out, sem):
+    copies = [
+        pltpu.make_async_copy(src, dst, sem.at[i])
+        for i, (src, dst) in enumerate(((a, a_out), (b, b_out), (c, c_out)))
+    ]
+    for copy in copies:
+        copy.start()
+    for copy in copies:
+        copy.wait()
 
 
 def per_device(

time: 27.3 us -> 19.6 us (0.72)
  local copies, waits for them, and re-layouts: 8.29 us -> 0 us
  Pallas kernels: 17.9 us -> 18.7 us
    unnamed x19 -> x0, local copies, waits for them, and re-layouts: 8.29 us -> none
    pallas_call x0 -> x1, Pallas kernels: none -> 0.73 us  [fused(): pl.pallas_call(store_kernel, out_shape=tuple((jax.ShapeDtypeStruct(part.s...]
where the time goes in v2:
time: 19.6 us; the launch traced here: 19.4 us
  Pallas kernels  18.7 us (95%)
  between operations  0.64 us (3%)
    pallas_call x1, Pallas kernels, fused(): pl.pallas_call(functools.partial(fused_kernel, n, m), out_shape=(jax.Shap...  18 us
    pallas_call x1, Pallas kernels, fused(): pl.pallas_call(store_kernel, out_shape=tuple((jax.ShapeDtypeStruct(part.s...  0.73 us

profile of v2, /device:TPU:0, one launch (start us, length us, event | category | flops | bytes accessed | tf_op | source)
XLA Modules:
  0.0 19.4 jit_solution(10046976789640541176)
XLA Ops:
  0.6 18.0 %shard_map.103 = (bf16[64,1024]{1,0:T(8,128)(2,1)S(1)}, bf16[64,1024]{1,0:T(8,128)(2,1)S(1)}, f32[8,64]{1,0:T(8,128)S(1)}) custom-call(bf16[64,1024]{1,0:T(8,128)(2,1)} %q_in.1, bf16[64,1024]{1,0:T(8,128)(2,1)} %k_in.1, bf16[64,1024]{1,0:T(8,128)(2,1)} %v_in.1, f32[8,64]{1,0:T(8,128)} %ld_in.1, bf16[16,4096]{1,0:T(8,128)(2,1)} %qs_in.1, ...), custom_call_target="tpu_custom_call" | custom-call | tf_op jit(solution)/shard_map/pallas_call | solution.py:377
  18.6 0.7 %shard_map.104 = (bf16[64,1024]{1,0:T(8,128)(2,1)}, bf16[64,1024]{1,0:T(8,128)(2,1)}, f32[8,64]{1,0:T(8,128)}) custom-call(bf16[64,1024]{1,0:T(8,128)(2,1)S(1)} %get-tuple-element.6.a, bf16[64,1024]{1,0:T(8,128)(2,1)S(1)} %get-tuple-element.7.b, f32[8,64]{1,0:T(8,128)S(1)} %get-tuple-element.8.c), custom_call_target="tpu_custom_call" | custom-call | tf_op jit(solution)/shard_map/pallas_call | solution.py:412

commit v3 on v2

--- a/solution.py
+++ b/solution.py
@@ -159,7 +159,7 @@
 def fused_kernel(
     n, m, q_in, k_in, v_in, ld_in, qs_in, ks_in, vs_in, doc_in,
     lin_out, soft_out, lse_out,
-    stage, lin_all, aux, aux_all, ld_v, doc_v, qs, kv, lin_v, soft_v, lse_v, bias,
+    stage, lin_all, aux, aux_all, ld_v, doc_v, qs, kvs, kv, lin_v, soft_v, lse_v, bias,
     loc_sem, lin_s, lin_r, aux_s, aux_r, kv1_s, kv1_r, qs_s, qs_r, kv2_s, kv2_r, out_s, out_r,
 ):
     span, heads = doc_in.shape[1], ld_in.shape[0]
@@ -167,13 +167,17 @@
     tokens = n * span
     me, hd = lax.axis_index("seq"), lax.axis_index("head")
 
+    kv[...] = jnp.zeros_like(kv)
     barrier = pltpu.get_barrier_semaphore()
-    seq_peers = [lax.rem(me + j, n) for j in range(1, n)]
+    pair, core = me // 2, lax.rem(me, 2)
+    far = [n // 2 - 1 - pair, pair + 1 - 2 * lax.rem(pair, 2)]
+    far += [lax.rem(pair + j, n // 2) for j in range(2, n // 2, 2)]
+    seq_peers = [2 * other + c for other in far for c in (core, 1 - core)] + [me + 1 - 2 * core]
     head_peers = [lax.rem(hd + j, m) for j in range(1, m)]
+    for peer in head_peers:
+        pl.semaphore_signal(barrier, inc=1, device_id={"head": peer}, device_id_type=MESH)
     for peer in seq_peers:
         pl.semaphore_signal(barrier, inc=1, device_id={"seq": peer}, device_id_type=MESH)
-    for peer in head_peers:
-        pl.semaphore_signal(barrier, inc=1, device_id={"head": peer}, device_id_type=MESH)
 
     def cols(index, width=DH):
         return pl.ds(pl.multiple_of(index * width, width), width)
@@ -187,12 +191,8 @@
         pltpu.make_async_copy(q_in, stage.at[0], loc_sem.at[2]),
         pltpu.make_async_copy(k_in, stage.at[1], loc_sem.at[3]),
         pltpu.make_async_copy(v_in, stage.at[2], loc_sem.at[4]),
-        pltpu.make_async_copy(
-            ks_in.at[:, cols(hd)], kv.at[0, own_rows(me * m + hd, rows), :], loc_sem.at[5]
-        ),
-        pltpu.make_async_copy(
-            vs_in.at[:, cols(hd)], kv.at[1, own_rows(me * m + hd, rows), :], loc_sem.at[6]
-        ),
+        pltpu.make_async_copy(ks_in, kvs.at[0], loc_sem.at[5]),
+        pltpu.make_async_copy(vs_in, kvs.at[1], loc_sem.at[6]),
         pltpu.make_async_copy(
             qs_in.at[:, cols(hd, heads * DH)], qs.at[own_rows(hd, rows), :], loc_sem.at[7]
         ),
@@ -205,8 +205,12 @@
     aux[0:heads, 0:span] = ld_v[...]
     aux[heads : heads + 1, 0:span] = doc_v[...].astype(jnp.float32)
     aux_all[me] = aux[...]
-    for load in loads[2:5]:
+    for load in loads[2:7]:
         load.wait()
+    own_kv = pltpu.make_async_copy(
+        kvs.at[:, :, cols(hd)], kv.at[:, own_rows(me * m + hd, rows), :], loc_sem.at[5]
+    )
+    own_kv.start()
     own = pltpu.make_async_copy(
         stage.at[:, :, cols(me)], lin_all.at[:, own_rows(me, span), :], loc_sem.at[8]
     )
@@ -221,14 +225,12 @@
 
     kv1, qsc = [], []
     for j, peer in enumerate(head_peers):
-        dst_rows = own_rows(me * m + hd, rows)
-        for side, src in enumerate((ks_in, vs_in)):
-            kv1.append(
-                remote(
-                    src.at[:, cols(peer)], kv.at[side, dst_rows, :],
-                    kv1_s.at[2 * j + side], kv1_r.at[2 * j + side], {"head": peer},
-                )
+        kv1.append(
+            remote(
+                kvs.at[:, :, cols(peer)], kv.at[:, own_rows(me * m + hd, rows), :],
+                kv1_s.at[j], kv1_r.at[j], {"head": peer},
             )
+        )
         qsc.append(
             remote(
                 qs_in.at[:, cols(peer, heads * DH)], qs.at[own_rows(hd, rows), :],
@@ -236,36 +238,56 @@
             )
         )
     auxc = [
-        remote(aux, aux_all.at[me], aux_s.at[j], aux_r.at[j], {"seq": peer})
+        remote(aux, aux_all.at[me], aux_s.at[j], aux_r.at[me], {"seq": peer})
         for j, peer in enumerate(seq_peers)
     ]
     linc = [
         remote(
             stage.at[:, :, cols(peer)], lin_all.at[:, own_rows(me, span), :],
-            lin_s.at[j], lin_r.at[j], {"seq": peer},
+            lin_s.at[j], lin_r.at[me], {"seq": peer},
         )
         for j, peer in enumerate(seq_peers)
     ]
     mine = kv.at[:, own_rows(me, span), :]
     kv2 = [
-        remote(mine, mine, kv2_s.at[j], kv2_r.at[j], {"seq": peer})
+        remote(mine, mine, kv2_s.at[j], kv2_r.at[me], {"seq": peer})
         for j, peer in enumerate(seq_peers)
     ]
-    outc = [
-        remote(
-            lin_v.at[own_rows(peer, span), :], lin_out.at[:, cols(me)],
-            out_s.at[j], out_r.at[j], {"seq": peer},
-        )
-        for j, peer in enumerate(seq_peers)
-    ]
-    for copy in kv1 + auxc + linc + qsc:
+
+    def result_to(block):
+        return remote(
+            lin_v.at[block * span : (block + 1) * span, :], lin_out.at[:, cols(me)],
+            out_s.at[block], out_r.at[me], {"seq": block},
+        )
+
+    def arrived(copy_from, source):
+        @pl.when(source != me)
+        def _():
+            copy_from(source).wait_recv()
+
+    def aux_from(source):
+        return remote(aux, aux_all.at[source], aux_s.at[0], aux_r.at[source], {"seq": source})
+
+    def lin_from(source):
+        here = lin_all.at[:, source * span : (source + 1) * span, :]
+        return remote(here, here, lin_s.at[0], lin_r.at[source], {"seq": source})
+
+    def out_from(source):
+        here = lin_out.at[:, source * DH : (source + 1) * DH]
+        return remote(here, here, out_s.at[0], out_r.at[source], {"seq": source})
+
+    for copy in kv1:
         copy.start()
-    loads[5].wait()
-    loads[6].wait()
+    for small, large in zip(auxc, linc):
+        small.start()
+        large.start()
+    for copy in qsc:
+        copy.start()
+    own_kv.wait()
     for copy in kv1:
         copy.wait_recv()
-    for copy in kv2:
-        copy.start()
+    for copy, peer in zip(kv2, seq_peers):
+        pl.when(peer > me)(copy.start)
 
     def iota(shape, dim):
         return lax.broadcasted_iota(jnp.int32, shape, dim)
@@ -279,8 +301,8 @@
     bias[0:span, :] = half
     bias[span : 2 * span, :] = half
 
-    for copy in auxc:
-        copy.wait_recv()
+    for source in range(n):
+        arrived(aux_from, source)
     blk = 2 * span
     eye = iota((blk, blk), 0) == iota((blk, blk), 1)
     tri = iota((blk, blk), 0) >= iota((blk, blk), 1)
@@ -300,9 +322,9 @@
         doc_cols.append(jnp.sum(jnp.where(eye, docs, 0.0), axis=1, keepdims=True).astype(jnp.int32))
 
     own.wait()
-    for copy in linc:
-        copy.wait_recv()
     for i in range(tokens // blk):
+        arrived(lin_from, 2 * i)
+        arrived(lin_from, 2 * i + 1)
         here = slice(i * blk, (i + 1) * blk)
         reach = (i + 1) * blk
         score = lax.dot_general(
@@ -320,16 +342,23 @@
         )
         normed = out * lax.rsqrt(jnp.mean(out * out, axis=1, keepdims=True) + 1e-06)
         lin_v[here, :] = normed.astype(jnp.bfloat16)
-    for copy in outc:
-        copy.start()
+        for block in (2 * i, 2 * i + 1):
+            pl.when(block != me)(result_to(block).start)
     own_out = pltpu.make_async_copy(
         lin_v.at[own_rows(me, span), :], lin_out.at[:, cols(me)], loc_sem.at[9]
     )
     own_out.start()
 
     loads[7].wait()
-    for copy in qsc + kv2:
+    for copy in qsc:
         copy.wait_recv()
+    for source in range(n - 1):
+
+        @pl.when(source < me)
+        def _():
+            here = kv.at[:, source * span : (source + 1) * span, :]
+            remote(here, here, kv2_s.at[0], kv2_r.at[source], {"seq": source}).wait_recv()
+
     stores = []
     for i in range(heads // 2):
         queries = jnp.concatenate(
@@ -358,13 +387,17 @@
     stores.append(pltpu.make_async_copy(lse_v, lse_out, loc_sem.at[10 + heads // 2]))
     stores[-1].start()
 
-    for copy in outc:
-        copy.wait_recv()
+    for source in range(n):
+        arrived(out_from, source)
     own_out.wait()
     for copy in stores:
         copy.wait()
-    for copy in kv1 + auxc + linc + qsc + kv2 + outc:
+    for copy in kv1 + auxc + linc + qsc:
         copy.wait_send()
+    for copy, peer in zip(kv2, seq_peers):
+        pl.when(peer > me)(copy.wait_send)
+    for block in range(n):
+        pl.when(block != me)(result_to(block).wait_send)
 
 
 def fused(n, m, query_lin, key_lin, value_lin, log_decay, query_soft, key_soft, value_soft, doc_start):
@@ -391,6 +424,7 @@
             pltpu.VMEM((heads, span), f32),
             pltpu.VMEM((1, span), jnp.int32),
             pltpu.VMEM((span, heads * DH), bf16),
+            pltpu.VMEM((2, rows, m * DH), bf16),
             pltpu.VMEM((2, tokens, DH), bf16),
             pltpu.VMEM((tokens, DH), bf16),
             pltpu.VMEM((span, heads * DH), bf16),
@@ -398,10 +432,9 @@
             pltpu.VMEM((2 * span, tokens), f32),
             dma((11 + heads // 2,)),
         ]
-        + [dma((n - 1,))] * 4
-        + [dma((2 * (m - 1),))] * 2
-        + [dma((m - 1,))] * 2
-        + [dma((n - 1,))] * 4,
+        + [dma((n,))] * 4
+        + [dma((m - 1,))] * 4
+        + [dma((n,))] * 4,
         compiler_params=pltpu.CompilerParams(
             collective_id=0, has_side_effects=True, vmem_limit_bytes=32 * 1024 * 1024
         ),
@@ -434,7 +467,7 @@
 ):
     n, m = lax.axis_size("seq"), lax.axis_size("head")
     span, heads = query_lin.shape[0], log_decay.shape[0]
-    if heads == n and span == DH // 2 and key_soft.shape[1] == m * DH and n % 2 == 0:
+    if heads == n == 8 and span == DH // 2 and key_soft.shape[1] == m * DH:
         return fused(
             n, m, query_lin, key_lin, value_lin, log_decay,
             query_soft, key_soft, value_soft, doc_start,

time: 19.6 us -> 18.2 us (0.929)
  Pallas kernels: 18.7 us -> 17.4 us
    pallas_call x1, Pallas kernels: 18 us -> 16.7 us  [fused(): pl.pallas_call(functools.partial(fused_kernel, n, m), out_shape=(jax.Shap...]
where the time goes in v3:
time: 18.2 us; the launch traced here: 18.1 us
  Pallas kernels  17.4 us (96%)
  between operations  0.64 us (4%)
    pallas_call x1, Pallas kernels, fused(): pl.pallas_call(functools.partial(fused_kernel, n, m), out_shape=(jax.Shap...  16.7 us
    pallas_call x1, Pallas kernels, fused(): pl.pallas_call(store_kernel, out_shape=tuple((jax.ShapeDtypeStruct(part.s...  0.73 us

profile of v3, /device:TPU:0, one launch (start us, length us, event | category | flops | bytes accessed | tf_op | source)
XLA Modules:
  0.0 18.1 jit_solution(9083456061122286962)
XLA Ops:
  0.6 16.7 %shard_map.103 = (bf16[64,1024]{1,0:T(8,128)(2,1)S(1)}, bf16[64,1024]{1,0:T(8,128)(2,1)S(1)}, f32[8,64]{1,0:T(8,128)S(1)}) custom-call(bf16[64,1024]{1,0:T(8,128)(2,1)} %q_in.1, bf16[64,1024]{1,0:T(8,128)(2,1)} %k_in.1, bf16[64,1024]{1,0:T(8,128)(2,1)} %v_in.1, f32[8,64]{1,0:T(8,128)} %ld_in.1, bf16[16,4096]{1,0:T(8,128)(2,1)} %qs_in.1, ...), custom_call_target="tpu_custom_call" | custom-call | tf_op jit(solution)/shard_map/pallas_call | solution.py:410
  17.3 0.7 %shard_map.104 = (bf16[64,1024]{1,0:T(8,128)(2,1)}, bf16[64,1024]{1,0:T(8,128)(2,1)}, f32[8,64]{1,0:T(8,128)}) custom-call(bf16[64,1024]{1,0:T(8,128)(2,1)S(1)} %get-tuple-element.6.a, bf16[64,1024]{1,0:T(8,128)(2,1)S(1)} %get-tuple-element.7.b, f32[8,64]{1,0:T(8,128)S(1)} %get-tuple-element.8.c), custom_call_target="tpu_custom_call" | custom-call | tf_op jit(solution)/shard_map/pallas_call | solution.py:445

commit v4 on v3

--- a/solution.py
+++ b/solution.py
@@ -276,12 +276,7 @@
         here = lin_out.at[:, source * DH : (source + 1) * DH]
         return remote(here, here, out_s.at[0], out_r.at[source], {"seq": source})
 
-    for copy in kv1:
-        copy.start()
-    for small, large in zip(auxc, linc):
-        small.start()
-        large.start()
-    for copy in qsc:
+    for copy in auxc + kv1 + linc + qsc:
         copy.start()
     own_kv.wait()
     for copy in kv1:
@@ -387,17 +382,17 @@
     stores.append(pltpu.make_async_copy(lse_v, lse_out, loc_sem.at[10 + heads // 2]))
     stores[-1].start()
 
-    for source in range(n):
-        arrived(out_from, source)
-    own_out.wait()
-    for copy in stores:
-        copy.wait()
     for copy in kv1 + auxc + linc + qsc:
         copy.wait_send()
     for copy, peer in zip(kv2, seq_peers):
         pl.when(peer > me)(copy.wait_send)
     for block in range(n):
         pl.when(block != me)(result_to(block).wait_send)
+    for source in range(n):
+        arrived(out_from, source)
+    own_out.wait()
+    for copy in stores:
+        copy.wait()
 
 
 def fused(n, m, query_lin, key_lin, value_lin, log_decay, query_soft, key_soft, value_soft, doc_start):

time: 18.2 us -> 17.6 us (0.967)
  Pallas kernels: 17.4 us -> 16.7 us
    pallas_call x1, Pallas kernels: 16.7 us -> 16 us  [fused(): pl.pallas_call(functools.partial(fused_kernel, n, m), out_shape=(jax.Shap...]
where the time goes in v4:
time: 17.6 us; the launch traced here: 17.4 us
  Pallas kernels  16.7 us (95%)
  between operations  0.64 us (4%)
    pallas_call x1, Pallas kernels, fused(): pl.pallas_call(functools.partial(fused_kernel, n, m), out_shape=(jax.Shap...  16 us
    pallas_call x1, Pallas kernels, fused(): pl.pallas_call(store_kernel, out_shape=tuple((jax.ShapeDtypeStruct(part.s...  0.73 us

profile of v4, /device:TPU:0, one launch (start us, length us, event | category | flops | bytes accessed | tf_op | source)
XLA Modules:
  0.0 17.4 jit_solution(18087641181133681413)
XLA Ops:
  0.6 16.0 %shard_map.103 = (bf16[64,1024]{1,0:T(8,128)(2,1)S(1)}, bf16[64,1024]{1,0:T(8,128)(2,1)S(1)}, f32[8,64]{1,0:T(8,128)S(1)}) custom-call(bf16[64,1024]{1,0:T(8,128)(2,1)} %q_in.1, bf16[64,1024]{1,0:T(8,128)(2,1)} %k_in.1, bf16[64,1024]{1,0:T(8,128)(2,1)} %v_in.1, f32[8,64]{1,0:T(8,128)} %ld_in.1, bf16[16,4096]{1,0:T(8,128)(2,1)} %qs_in.1, ...), custom_call_target="tpu_custom_call" | custom-call | tf_op jit(solution)/shard_map/pallas_call | solution.py:405
  16.6 0.7 %shard_map.104 = (bf16[64,1024]{1,0:T(8,128)(2,1)}, bf16[64,1024]{1,0:T(8,128)(2,1)}, f32[8,64]{1,0:T(8,128)}) custom-call(bf16[64,1024]{1,0:T(8,128)(2,1)S(1)} %get-tuple-element.6.a, bf16[64,1024]{1,0:T(8,128)(2,1)S(1)} %get-tuple-element.7.b, f32[8,64]{1,0:T(8,128)S(1)} %get-tuple-element.8.c), custom_call_target="tpu_custom_call" | custom-call | tf_op jit(solution)/shard_map/pallas_call | solution.py:440

commit v5 on v4

--- a/solution.py
+++ b/solution.py
@@ -167,7 +167,6 @@
     tokens = n * span
     me, hd = lax.axis_index("seq"), lax.axis_index("head")
 
-    kv[...] = jnp.zeros_like(kv)
     barrier = pltpu.get_barrier_semaphore()
     pair, core = me // 2, lax.rem(me, 2)
     far = [n // 2 - 1 - pair, pair + 1 - 2 * lax.rem(pair, 2)]
@@ -205,16 +204,13 @@
     aux[0:heads, 0:span] = ld_v[...]
     aux[heads : heads + 1, 0:span] = doc_v[...].astype(jnp.float32)
     aux_all[me] = aux[...]
-    for load in loads[2:7]:
-        load.wait()
-    own_kv = pltpu.make_async_copy(
-        kvs.at[:, :, cols(hd)], kv.at[:, own_rows(me * m + hd, rows), :], loc_sem.at[5]
-    )
-    own_kv.start()
-    own = pltpu.make_async_copy(
-        stage.at[:, :, cols(me)], lin_all.at[:, own_rows(me, span), :], loc_sem.at[8]
-    )
-    own.start()
+    for block in range(1, n):
+
+        @pl.when(block > me)
+        def _():
+            part = slice(block * span, (block + 1) * span)
+            kv[:, part, :] = jnp.zeros((2, span, DH), kv.dtype)
+
     pl.semaphore_wait(barrier, n + m - 2)
 
     def remote(src, dst, send, recv, device):
@@ -276,7 +272,19 @@
         here = lin_out.at[:, source * DH : (source + 1) * DH]
         return remote(here, here, out_s.at[0], out_r.at[source], {"seq": source})
 
-    for copy in auxc + kv1 + linc + qsc:
+    for copy in auxc:
+        copy.start()
+    for load in loads[2:7]:
+        load.wait()
+    own_kv = pltpu.make_async_copy(
+        kvs.at[:, :, cols(hd)], kv.at[:, own_rows(me * m + hd, rows), :], loc_sem.at[5]
+    )
+    own_kv.start()
+    own = pltpu.make_async_copy(
+        stage.at[:, :, cols(me)], lin_all.at[:, own_rows(me, span), :], loc_sem.at[8]
+    )
+    own.start()
+    for copy in kv1 + linc + qsc:
         copy.start()
     own_kv.wait()
     for copy in kv1:

time: 17.6 us -> 17.6 us (level)
  no operation moved by 1% of the time
where the time goes in v5:
time: 17.6 us; the launch traced here: 17.4 us
  Pallas kernels  16.7 us (95%)
  between operations  0.64 us (4%)
    pallas_call x1, Pallas kernels, fused(): pl.pallas_call(functools.partial(fused_kernel, n, m), out_shape=(jax.Shap...  16 us
    pallas_call x1, Pallas kernels, fused(): pl.pallas_call(store_kernel, out_shape=tuple((jax.ShapeDtypeStruct(part.s...  0.73 us

profile of v5, /device:TPU:0, one launch (start us, length us, event | category | flops | bytes accessed | tf_op | source)
XLA Modules:
  0.0 17.4 jit_solution(14551096566372574971)
XLA Ops:
  0.6 16.0 %shard_map.103 = (bf16[64,1024]{1,0:T(8,128)(2,1)S(1)}, bf16[64,1024]{1,0:T(8,128)(2,1)S(1)}, f32[8,64]{1,0:T(8,128)S(1)}) custom-call(bf16[64,1024]{1,0:T(8,128)(2,1)} %q_in.1, bf16[64,1024]{1,0:T(8,128)(2,1)} %k_in.1, bf16[64,1024]{1,0:T(8,128)(2,1)} %v_in.1, f32[8,64]{1,0:T(8,128)} %ld_in.1, bf16[16,4096]{1,0:T(8,128)(2,1)} %qs_in.1, ...), custom_call_target="tpu_custom_call" | custom-call | tf_op jit(solution)/shard_map/pallas_call | solution.py:413
  16.6 0.7 %shard_map.104 = (bf16[64,1024]{1,0:T(8,128)(2,1)}, bf16[64,1024]{1,0:T(8,128)(2,1)}, f32[8,64]{1,0:T(8,128)}) custom-call(bf16[64,1024]{1,0:T(8,128)(2,1)S(1)} %get-tuple-element.6.a, bf16[64,1024]{1,0:T(8,128)(2,1)S(1)} %get-tuple-element.7.b, f32[8,64]{1,0:T(8,128)S(1)} %get-tuple-element.8.c), custom_call_target="tpu_custom_call" | custom-call | tf_op jit(solution)/shard_map/pallas_call | solution.py:448
